TPU v7x, 512 devices: a whole 4x4x16 slice. The times are simulated.
512 devices in a mesh: warp: 32 (over z_hi, x, core), weft: 16 (over y, z_lo).
Axes of the slice: x: 4, y: 4, z: 16 (z_hi: 4, z_lo: 4; z = z_hi * 4 + z_lo), core: 2. Of those that a mesh axis runs over, the one named last changes fastest.
Arguments:
- fabric_state: float32 [1, 8, 256, 2048], P(None, None, 'warp', 'weft'), may hold values from -3 to 3
- final_adjoint: float32 [1, 8, 256, 2048], P(None, None, 'warp', 'weft'), may hold values from -6 to 6
- stiffness: float32 [2, 256, 2048], P(None, 'warp', 'weft'), may hold values from 0.5 to 2
- pinned: int32 [1, 256, 2048], P(None, 'warp', 'weft'), may hold values 0 or 1
- weave_codes: int32 [256, 2048], P('warp', 'weft'), may hold values from 0 to 3
- first_weight: bfloat16 [12, 256], replicated, may hold values from -1.75 to 1.75
- second_weight: bfloat16 [256, 256], replicated, may hold values from -0.375 to 0.375
- third_weight: bfloat16 [256, 2], replicated, may hold values from -0.375 to 0.375
Outputs:
- final_state: float32 [1, 8, 256, 2048], P(None, None, 'warp', 'weft')
- state_adjoint: float32 [1, 8, 256, 2048], P(None, None, 'warp', 'weft')
- first_grad: float32 [12, 256], replicated
- second_grad: float32 [256, 256], replicated
- third_grad: float32 [256, 2], replicated
Inputs may be any that keep to these rules, and one draw needn't show every extreme that they name: `pinned`: 1 marks a crossing held fixed in that drape condition. `weave_codes`: bit 0 tells whether the warp passes over, bit 1 the weave's second pattern bit.
All inputs are finite; a program needn't handle non-finite values. No bound on the sum of `pinned` on one device may be relied on, other than what follows from the above.
Results may differ from a plain program's by a relative error of at most 0.0049.
Values sent between devices are 32-bit elements; how exact they have to be, the bound alone decides.
No kernel may reach another device: no remote copies, remote signals or barrier semaphores. Data moves between devices by JAX's collectives and lax.ppermute only.
A program may use at most 64 MiB of HBM per device.

v0:
```python
import functools

import jax
import jax.numpy as jnp
from jax import lax
from jax.experimental import pallas as pl
from jax.experimental.pallas import tpu as pltpu
from jax.sharding import Mesh, PartitionSpec as P

WARP = ("zhi", "x", "core")
WEFT = ("y", "zlo")
PLANE = ("x", "core", "y")
COLUMN = ("zhi", "zlo")

DT = 0.25
DAMP = 0.9
KB = 0.25
KC = 0.5
KS = 0.5
GRAV = 0.3

TILE_ROWS = 8
LANES = 128
REACH = 10
FIRST = REACH
ALL_ROWS = TILE_ROWS + 2 * REACH
HID = 256
OWN = TILE_ROWS * LANES
FEATURE_ROWS = (6, 7, 3, 4, 5, 14, 15, 8, 9, 2, 10, 11)
F32 = jnp.float32
BF16 = jnp.bfloat16


def span(radius):
    return range(FIRST - radius, FIRST + TILE_ROWS + radius)


def distance(row):
    return max(FIRST - row, row - (FIRST + TILE_ROWS - 1), 0)


def ring(e):
    return [FIRST - e, FIRST + TILE_ROWS - 1 + e]


class Plan:
    def __init__(self, reach, back):
        self.reach, self.back = reach, back
        own = list(range(FIRST, FIRST + TILE_ROWS))
        order = own + [r for e in range(1, back + 1) for r in ring(e)]
        near = len(order)
        order = order + [None] + [r for e in range(back + 1, reach + 1) for r in ring(e)]
        self.tile = {r: t for t, r in enumerate(order) if r is not None}
        self.forward, self.backward = {}, {}
        at = {near: 0, len(order): 0}

        def put(table, row, tile, width):
            table[row] = (tile, at[tile], width)
            at[tile] += 2 * width

        for r in own:
            put(self.forward, r, near, reach)
            self.backward[r] = self.forward[r]
        for e in range(1, reach):
            width, need = reach - e, back - e
            for r in ring(e):
                if need > 0 and at[near] + 2 * width <= LANES and (e == 1 or reach == back):
                    put(self.forward, r, near, width)
                    self.backward[r] = self.forward[r]
                else:
                    put(self.forward, r, len(order), width)
                    if need > 0:
                        put(self.backward, r, near, need)
        self.packed = {near} | ({len(order)} if at[len(order)] else set())
        assert max(at.values()) <= LANES
        self.near = near
        self.tiles = len(order) + (1 if at[len(order)] else 0)
        middle = {16: 16, 14: 15}.get(self.tiles - TILE_ROWS, self.tiles)
        self.saved = middle
        self.blocks = [(0, TILE_ROWS), (TILE_ROWS, middle)]
        if middle < self.tiles:
            self.blocks.append((middle, self.tiles))


PLANS = [Plan(7, 1), Plan(6, 3), Plan(5, 5)]


def dot(left, right):
    return lax.dot_general(left, right, (((1,), (0,)), ((), ())), preferred_element_type=F32)


def dot_columns(left, right):
    return lax.dot_general(left, right, (((0,), (0,)), ((), ())), preferred_element_type=F32)


def dot_rows(left, right):
    return lax.dot_general(left, right, (((1,), (1,)), ((), ())), preferred_element_type=F32)


def lane_index():
    return lax.broadcasted_iota(jnp.int32, (8, LANES), 1)


def field_index():
    return lax.broadcasted_iota(jnp.int32, (8, LANES), 0)


def pack_kernel(
    state_hbm, adjoint_hbm, stiff_hbm, pinned_hbm, weave_hbm, third_hbm,
    own_ref, low_ref, high_ref, last_ref,
    state_ref, adjoint_ref, stiff_ref, pinned_ref, weave_ref, third_ref, sems,
):
    sources = (state_hbm, adjoint_hbm, stiff_hbm, pinned_hbm, weave_hbm, third_hbm)
    targets = (state_ref, adjoint_ref, stiff_ref, pinned_ref, weave_ref, third_ref)
    copies = [pltpu.make_async_copy(a, b, sems.at[i]) for i, (a, b) in enumerate(zip(sources, targets))]
    for copy in copies:
        copy.start()
    for copy in copies:
        copy.wait()
    lane, field = lane_index(), field_index()
    last_ref[...] = jnp.zeros((1, 24, LANES), F32)
    third = third_ref[...].astype(F32)
    for f in range(2):
        last_ref[0, 2 * f : 2 * f + 1, :] = third[f : f + 1, 0:LANES]
        last_ref[0, 2 * f + 1 : 2 * f + 2, :] = third[f : f + 1, LANES:]
    low = [jnp.zeros((8, LANES), F32) for _ in range(3)]
    high = [jnp.zeros((8, LANES), F32) for _ in range(3)]
    for row in range(TILE_ROWS):
        k0 = stiff_ref[0, row : row + 1, :]
        k1 = stiff_ref[1, row : row + 1, :]
        free = 1.0 - pinned_ref[0, row : row + 1, :].astype(F32)
        code = weave_ref[row : row + 1, :]
        first_sign = (2 * jnp.bitwise_and(code, 1) - 1).astype(F32)
        second_sign = (2 * jnp.right_shift(code, 1) - 1).astype(F32)
        cell = jnp.where(field == 5, 1.0, 0.0)
        for place, value in enumerate((k0, k1, first_sign, second_sign, free)):
            cell = jnp.where(field == place, value, cell)
        at = REACH * row
        here = (lane >= at) & (lane < at + REACH)
        for part, value in enumerate((state_ref[0, :, row, :], adjoint_ref[0, :, row, :], cell)):
            own_ref[row, 8 * part : 8 * part + 8, :] = value
            low[part] = jnp.where(here, pltpu.roll(value, at, 1) if at else value, low[part])
            shift = (at + REACH) % LANES
            high[part] = jnp.where(here, pltpu.roll(value, shift, 1), high[part])
    for part in range(3):
        low_ref[8 * part : 8 * part + 8, :] = low[part]
        high_ref[8 * part : 8 * part + 8, :] = high[part]


def roll(value, shift, axis):
    shift = shift % value.shape[axis]
    return pltpu.roll(value, shift, axis) if shift else value


def main_kernel(
    own_ref,
    core_ref,
    partner_ref,
    cross_ref,
    far_ref,
    first_weight_ref,
    second_weight_ref,
    final_hbm,
    adjoint_hbm,
    grads_ref,
    final_ref,
    adjoint_ref,
    sems,
    state_a,
    state_b,
    later,
    adjoint,
    k0_ref,
    k1_ref,
    mask_ref,
    sign_ref,
    force_ref,
    ahead_ref,
    behind_ref,
    sum_ref,
    x0,
    x1,
    x2,
    slope_first0,
    slope_first1,
    slope_first2,
    slope_second0,
    slope_second1,
    slope_second2,
    act_first,
    act_second,
    friction,
    upstream,
    feature_back,
    total_second,
    total_first,
    total_third,
):
    lane, field = lane_index(), field_index()
    zero = jnp.zeros((8, LANES), F32)
    xs = (x0, x1, x2)
    slopes_first = (slope_first0, slope_first1, slope_first2)
    slopes_second = (slope_second0, slope_second1, slope_second2)
    f_row = lax.broadcasted_iota(jnp.int32, (16, 12), 0)
    f_column = lax.broadcasted_iota(jnp.int32, (16, 12), 1)
    chosen = jnp.zeros((16, 12), F32)
    for f, n in enumerate(FEATURE_ROWS):
        chosen = jnp.where((f_row == n) & (f_column == f), 1.0, chosen)
    w1_wide = dot(chosen.astype(BF16), first_weight_ref[...])
    w1, w1_half = w1_wide.astype(BF16), (0.5 * w1_wide).astype(BF16)
    w2 = (0.5 * second_weight_ref[...].astype(F32)).astype(BF16)
    f_row = lax.broadcasted_iota(jnp.int32, (16, 2), 0)
    f_column = lax.broadcasted_iota(jnp.int32, (16, 2), 1)
    third = [
        jnp.concatenate([own_ref[TILE_ROWS + 2, 2 * f + i : 2 * f + i + 1, :] for i in range(2)], axis=1)
        for f in range(2)
    ]
    third = jnp.concatenate(third, axis=0).astype(BF16)
    w3_wide = dot(jnp.where(f_row == f_column + 6, 1.0, 0.0).astype(BF16), third)
    w3t, w3 = w3_wide[0:8].astype(BF16), (0.5 * w3_wide).astype(BF16)
    place = field < 3
    speed = (field >= 3) & (field < 6)
    slide = field >= 6

    def beside(low, high, row):
        at = REACH * row
        out = jnp.where(lane < REACH, roll(high, -at, 1), 0.0)
        return jnp.where(lane >= LANES - REACH, roll(low, LANES - REACH - at, 1), out)

    first_core = core_ref[0] == 0

    def pick(lower, upper, at):
        return jnp.where(first_core, lower[at], upper[at])

    def received(e, part):
        at = slice(8 * part, 8 * part + 8)
        if e < -TILE_ROWS:
            i = e + TILE_ROWS + 2
            return [
                jnp.where(first_core, cross_ref[n, p, :], far_ref[m])
                for (n, p), m in zip(extra(i), (i, 2, 3))
            ]
        if e < 0:
            return [pick(cross_ref, partner_ref, (i, at)) for i in (e + TILE_ROWS, TILE_ROWS, TILE_ROWS + 1)]
        if e < TILE_ROWS:
            return [own_ref[i, at, :] for i in (e, TILE_ROWS, TILE_ROWS + 1)]
        if e < 2 * TILE_ROWS:
            return [pick(partner_ref, cross_ref, (i, at)) for i in (e - TILE_ROWS, TILE_ROWS, TILE_ROWS + 1)]
        i = e - 2 * TILE_ROWS
        return [
            jnp.where(first_core, far_ref[m], cross_ref[n, p, :])
            for (n, p), m in zip(extra(i), (i, 2, 3))
        ]

    def extra(i):
        n = TILE_ROWS + 2
        row = (n, slice(8 * i, 8 * i + 8))
        return row, (n, slice(16, 24)), (n + 1, slice(0, 8))

    for row in range(ALL_ROWS):
        e = row - FIRST
        near = e % TILE_ROWS
        for part in range(3 if -TILE_ROWS <= e < 2 * TILE_ROWS else 1):
            value, low, high = received(e, part)
            pair = (value, beside(low, high, near))
            for half in range(2):
                value = pair[half]
                if part == 0:
                    state_a[row, half] = value
                elif part == 1:
                    adjoint[row, half] = value
                else:
                    k0_ref[row, half] = jnp.broadcast_to(value[0:1], (8, LANES))
                    k1_ref[row, half] = jnp.broadcast_to(value[1:2], (8, LANES))
                    mask_ref[row, half] = jnp.where(
                        place, 1.0, jnp.where(speed, value[4:5], value[5:6])
                    )
                    sign_ref[row, half] = jnp.where((field == 2) | (field == 3), value, 0.0)

    def across(pair, step):
        turned = [roll(value, -step, 1) for value in pair]
        edge = lane >= LANES - step if step > 0 else lane < -step
        return jnp.where(edge, turned[1], turned[0]), jnp.where(edge, turned[0], turned[1])

    def both(ref, row):
        return ref[row, 0], ref[row, 1]

    def gather(total, value, entry):
        _, at, width = entry
        turned = roll(value, at + width, 1)
        return jnp.where((lane >= at) & (lane < at + 2 * width), turned, total)

    def scatter(value, entry):
        _, at, width = entry
        turned = roll(value, -(at + width), 1)
        return jnp.where((lane < width) | (lane >= LANES - width), turned, 0.0)

    def tile_lanes(tile):
        return slice(tile * LANES, (tile + 1) * LANES)

    gravity = jnp.where(field == 5, -GRAV, 0.0)
    keep = jnp.where(speed, DAMP, 1.0)

    def forward(k, state, target):
        plan = PLANS[k]
        x_ref = xs[k]
        moved = span((8, 6, 0)[k])
        packed = {tile: [zero, zero] for tile in plan.packed}
        for row in sorted(set(moved) | set(span(plan.reach))):
            here, up, down = both(state, row), both(state, row + 1), both(state, row - 1)
            right, left = across(here, 1), across(here, -1)
            update = row in moved
            if update:
                up2, down2 = both(state, row + 2), both(state, row - 2)
                right2, left2 = across(here, 2), across(here, -2)
            for half in range(2):
                s = here[half]
                twice = 2.0 * s
                lap_rows = up[half] + down[half] - twice
                lap_columns = right[half] + left[half] - twice
                slope_rows = 0.5 * (up[half] - down[half])
                slope_columns = 0.5 * (right[half] - left[half])
                if row in plan.tile:
                    mixed = jnp.where(field == 0, slope_rows, sign_ref[row, half])
                    mixed = jnp.where(field == 1, slope_columns, mixed)
                    mixed = jnp.where(field == 6, lap_rows, mixed)
                    mixed = jnp.where(field == 7, lap_columns, mixed)
                    if half == 0:
                        x_ref[:, tile_lanes(plan.tile[row])] = jnp.concatenate([s, mixed], axis=0).astype(BF16)
                    else:
                        for table in (plan.forward, plan.backward):
                            if row in table and (table is plan.forward or table[row] != plan.forward.get(row)):
                                entry = table[row]
                                old = packed[entry[0]]
                                packed[entry[0]] = [gather(old[0], s, entry), gather(old[1], mixed, entry)]
                if update and (half == 0 or k < 2):
                    bend = (up2[half] + down2[half] + right2[half] + left2[half]) - 4.0 * (
                        up[half] + down[half] + right[half] + left[half]
                    )
                    bend = bend + 12.0 * s
                    pull = k0_ref[row, half] * lap_rows + k1_ref[row, half] * lap_columns - KB * bend
                    turn = KC * jnp.where(field == 6, slope_rows, jnp.where(field == 7, slope_columns, 0.0))
                    force = roll(pull, 3, 0) + roll(turn, 5, 0) + gravity
                    rate = KS * jnp.where(field == 6, lap_rows, lap_columns)
                    change = jnp.where(speed, force, jnp.where(slide, rate, 0.0))
                    later[row, half] = keep * s + DT * change
        for tile, (top, bottom) in packed.items():
            x_ref[:, tile_lanes(tile)] = jnp.concatenate([top, bottom], axis=0).astype(BF16)

        def layer(z, keep_slope, block):
            bent = jnp.tanh(z)
            part = z * bent
            start, stop = block[0] * LANES, min(block[1], plan.saved) * LANES
            if stop > start:
                keep_slope[start:stop, :] = (1.0 + bent) * (1.0 + (z - part))
            return (z + part).astype(BF16)

        for block in plan.blocks:
            at = slice(block[0] * LANES, block[1] * LANES)
            act = layer(dot_columns(x_ref[:, at], w1_half), slopes_first[k], block)
            if block[0] == 0:
                act_first[k] = act
            act = layer(dot(act, w2), slopes_second[k], block)
            if block[0] == 0:
                act_second[k] = act
            if k < 2 or block[0] == 0:
                friction[:, at] = dot_rows(w3t, act)
        for row in moved:
            for half in range(2 if k < 2 else 1):
                value = later[row, half]
                if half == 0 and row in plan.tile:
                    value = value - DT * friction[:, tile_lanes(plan.tile[row])]
                if half == 1 and row in plan.forward:
                    entry = plan.forward[row]
                    value = value - DT * scatter(friction[:, tile_lanes(entry[0])], entry)
                value = mask_ref[row, half] * value
                value = value + jnp.where(place, DT * roll(value, 5, 0), 0.0)
                if k < 2:
                    target[row, half] = value
                else:
                    final_ref[0, :, row - FIRST, :] = value

    forward(0, state_a, state_b)
    forward(1, state_b, state_a)
    forward(2, state_a, None)
    final_copy = pltpu.make_async_copy(final_ref, final_hbm, sems.at[0])
    final_copy.start()

    def backward(k):
        plan = PLANS[k]
        inner, middle, outer = plan.back - 1, plan.back, plan.back + 1
        packed = zero
        for row in span(middle):
            for half in range(2):
                value = jnp.where(slide, -DT * adjoint[row, half], 0.0)
                if half == 0:
                    upstream[:, tile_lanes(plan.tile[row])] = jnp.concatenate([value, zero], axis=0).astype(BF16)
                elif row in plan.backward:
                    packed = gather(packed, value, plan.backward[row])
        upstream[:, tile_lanes(plan.near)] = jnp.concatenate([packed, zero], axis=0).astype(BF16)
        for start, stop in ((0, TILE_ROWS), (TILE_ROWS, plan.near + 1)):
            at = slice(start * LANES, stop * LANES)
            second_back = (dot_columns(upstream[:, at], w3) * slopes_second[k][at, :]).astype(BF16)
            first_back = (dot_rows(second_back, w2) * slopes_first[k][at, :]).astype(BF16)
            feature_back[:, at] = dot_rows(w1, first_back)
            if start == 0:
                second = dot_columns(act_first[k], second_back)
                first = dot(xs[k][:, at], first_back)
                third = dot(upstream[:, at], act_second[k])
        if k == 2:
            total_second[...], total_first[...], total_third[...] = second, first, third
        else:
            total_second[...] += second
            total_first[...] += first
            total_third[...] += third

        for row in span(outer):
            for half in range(2):
                q = adjoint[row, half]
                total = mask_ref[row, half] * (q + DT * roll(q, 3, 0))
                force_ref[row, half] = jnp.where(place, DT * roll(total, 5, 0), 0.0)
                if distance(row) <= inner:
                    sum_ref[row, half] = jnp.where(speed, DAMP * total, q)
        for row in span(middle):
            force = both(force_ref, row)
            high, low = [], []
            for half in range(2):
                q, g = adjoint[row, half], force[half]
                if half == 0:
                    at = tile_lanes(plan.tile[row])
                    straight, mixed = feature_back[0:8, at], feature_back[8:16, at]
                elif row in plan.backward:
                    entry = plan.backward[row]
                    at = tile_lanes(entry[0])
                    straight, mixed = scatter(feature_back[0:8, at], entry), scatter(feature_back[8:16, at], entry)
                else:
                    straight, mixed = zero, zero
                carried = DT * KS * q + mixed
                by_rows = k0_ref[row, half] * g + jnp.where(field == 6, carried, 0.0)
                by_columns = k1_ref[row, half] * g + jnp.where(field == 7, carried, 0.0)
                tilt = 0.5 * jnp.where(slide, KC * roll(g, 6, 0), mixed)
                tilt_rows = jnp.where((field == 0) | (field == 6), tilt, 0.0)
                tilt_columns = jnp.where((field == 1) | (field == 7), tilt, 0.0)
                ahead_ref[row, half] = by_rows + 4.0 * KB * g - tilt_rows
                behind_ref[row, half] = by_rows + 4.0 * KB * g + tilt_rows
                high.append(by_columns + 4.0 * KB * g - tilt_columns)
                low.append(by_columns + 4.0 * KB * g + tilt_columns)
                if distance(row) <= inner:
                    center = -2.0 * (by_rows + by_columns) - 12.0 * KB * g
                    sum_ref[row, half] = sum_ref[row, half] + straight + center
            if distance(row) <= inner:
                right, left = across(high, 1), across(low, -1)
                right2, left2 = across(force, 2), across(force, -2)
                for half in range(2):
                    sideways = right[half] + left[half] - KB * (right2[half] + left2[half])
                    sum_ref[row, half] = sum_ref[row, half] + sideways
        for row in span(inner):
            for half in range(2 if k > 0 else 1):
                value = sum_ref[row, half] + ahead_ref[row + 1, half] + behind_ref[row - 1, half]
                value = value - KB * (force_ref[row + 2, half] + force_ref[row - 2, half])
                if k > 0:
                    adjoint[row, half] = jnp.where(slide, mask_ref[row, half] * value, value)
                else:
                    adjoint_ref[0, :, row - FIRST, :] = value

    backward(2)
    backward(1)
    backward(0)
    adjoint_copy = pltpu.make_async_copy(adjoint_ref, adjoint_hbm, sems.at[1])
    adjoint_copy.start()

    small = total_first[...]
    third = total_third[0:8, :]
    row_index = lax.broadcasted_iota(jnp.int32, (8, HID), 0)
    top = jnp.where(row_index < 2, pltpu.roll(third, 2, 0), small[0:8])
    bottom = small[8:16]
    for c in range(HID // 8):
        for j in range(8):
            at = 8 * c + (2 * j) % 8
            side = slice(0, LANES) if j < 4 else slice(LANES, HID)
            grads_ref[c, j] = total_second[at : at + 2, side]
        line = (top if c < 16 else bottom)[(c // 2) % 8 : (c // 2) % 8 + 1, (c % 2) * LANES : (c % 2 + 1) * LANES]
        grads_ref[c, 8] = jnp.broadcast_to(line, (2, LANES))
    final_copy.wait()
    adjoint_copy.wait()


def run_main(*operands):
    rows = (ALL_ROWS, 2, 8, LANES)
    scratch = [pltpu.VMEM((1, 8, TILE_ROWS, LANES), F32)] * 2 + [pltpu.SemaphoreType.DMA((2,))]
    scratch += [pltpu.VMEM(rows, F32) for _ in range(12)]
    scratch += [pltpu.VMEM((16, plan.tiles * LANES), BF16) for plan in PLANS]
    scratch += [pltpu.VMEM((plan.saved * LANES, HID), F32) for plan in PLANS] * 2
    scratch += [pltpu.VMEM((3, OWN, HID), BF16)] * 2
    scratch += [
        pltpu.VMEM((8, PLANS[0].tiles * LANES), F32),
        pltpu.VMEM((16, PLANS[2].tiles * LANES), BF16),
        pltpu.VMEM((16, PLANS[2].tiles * LANES), F32),
        pltpu.VMEM((HID, HID), F32),
        pltpu.VMEM((16, HID), F32),
        pltpu.VMEM((16, HID), F32),
    ]
    return pl.pallas_call(
        main_kernel,
        out_shape=(
            jax.ShapeDtypeStruct((1, 8, TILE_ROWS, LANES), F32),
            jax.ShapeDtypeStruct((1, 8, TILE_ROWS, LANES), F32),
            jax.ShapeDtypeStruct((HID // 8, 9, 2, LANES), F32),
        ),
        in_specs=[pl.BlockSpec(memory_space=pltpu.SMEM if i == 1 else pltpu.VMEM) for i in range(len(operands))],
        out_specs=[pl.BlockSpec(memory_space=m) for m in (pltpu.HBM, pltpu.HBM, pltpu.VMEM)],
        scratch_shapes=scratch,
        compiler_params=pltpu.CompilerParams(vmem_limit_bytes=40 << 20),
        name="substeps",
    )(*operands)


def run_pack(*operands):
    return pl.pallas_call(
        pack_kernel,
        out_shape=(
            jax.ShapeDtypeStruct((TILE_ROWS, 24, LANES), F32),
            jax.ShapeDtypeStruct((24, LANES), F32),
            jax.ShapeDtypeStruct((24, LANES), F32),
            jax.ShapeDtypeStruct((1, 24, LANES), F32),
        ),
        in_specs=[pl.BlockSpec(memory_space=pltpu.HBM)] * 6,
        scratch_shapes=[pltpu.VMEM(value.shape, value.dtype) for value in operands]
        + [pltpu.SemaphoreType.DMA((6,))],
        name="pack_tile",
    )(*operands)


def shift(value, axis, step):
    count = lax.axis_size(axis)
    return lax.ppermute(value, axis, [(i, i + step) for i in range(count) if 0 <= i + step < count])


def sum_everywhere(part):
    plane, column = lax.axis_size(PLANE), lax.axis_size(COLUMN)
    part = jnp.sum(lax.all_to_all(part, PLANE, 0, 0, tiled=True), axis=0)
    part = jnp.broadcast_to(part, (column,) + part.shape)
    part = jnp.sum(lax.all_to_all(part, COLUMN, 0, 0, tiled=True), axis=0)
    part = jnp.broadcast_to(part, (plane,) + part.shape)
    return lax.all_to_all(part, PLANE, 0, 0, tiled=True)


def finish_kernel(scale, flat_ref, first_ref, second_ref, third_ref):
    for c in range(HID // 8):
        for j in range(8):
            at = 8 * c + (2 * j) % 8
            side = slice(0, LANES) if j < 4 else slice(LANES, HID)
            second_ref[at : at + 2, side] = flat_ref[c, j] * scale
    for half in range(2):
        at = slice(half * LANES, (half + 1) * LANES)
        for f, row in enumerate(FEATURE_ROWS):
            first_ref[f : f + 1, at] = flat_ref[2 * row + half, 8, 0:1, :] * scale
        for f in range(2):
            third_ref[f : f + 1, at] = flat_ref[2 * f + half, 8, 0:1, :] * scale


def shards(state, adjoint, stiffness, pinned, weave, first_weight, second_weight, third_weight):
    own, low_edge, high_edge, last = run_pack(state, adjoint, stiffness, pinned, weave, third_weight.T)
    left = shift(high_edge, WEFT, 1)
    right = shift(low_edge, WEFT, -1)
    own = jnp.concatenate([own, left[None], right[None], last], axis=0)
    count = lax.axis_size(WARP)
    core = lax.axis_index(WARP) % 2
    mates = [(i, i ^ 1) for i in range(count)]
    partner = lax.ppermute(own, WARP, mates)
    outward = lax.dynamic_slice_in_dim(partner, core * (TILE_ROWS - 2), 2, axis=0)[:, 0:8]
    tail = jnp.concatenate([outward, partner[TILE_ROWS : TILE_ROWS + 2, 0:8], jnp.zeros((2, 8, LANES), F32)], axis=0)
    wide = jnp.concatenate([own[: TILE_ROWS + 2], tail.reshape(2, 24, LANES)], axis=0)
    pairs = [(i, j) for i in range(count) for j in [((i + 1) ^ 1) - 1] if 0 <= j < count]
    cross = lax.ppermute(wide, WARP, pairs)
    inward = lax.dynamic_slice_in_dim(cross, (1 - core) * (TILE_ROWS - 2), 2, axis=0)[:, 0:8]
    far = lax.ppermute(jnp.concatenate([inward, cross[TILE_ROWS : TILE_ROWS + 2, 0:8]], axis=0), WARP, mates)

    final_state, state_adjoint, grads = run_main(
        own, core.reshape(1), partner, cross, far, first_weight, second_weight
    )
    flat = sum_everywhere(grads)
    cells = OWN * lax.axis_size(WARP) * lax.axis_size(WEFT)
    first, second, third = pl.pallas_call(
        functools.partial(finish_kernel, float(cells) ** -0.5),
        out_shape=(
            jax.ShapeDtypeStruct((12, HID), F32),
            jax.ShapeDtypeStruct((HID, HID), F32),
            jax.ShapeDtypeStruct((2, HID), F32),
        ),
        compiler_params=pltpu.CompilerParams(vmem_limit_bytes=4 << 20),
        name="unpack_grads",
    )(flat)
    return final_state, state_adjoint, first, second, third.T


def factors(mesh):
    warp, weft = mesh.shape["warp"], mesh.shape["weft"]
    zlo = 4 if weft % 4 == 0 else 1
    x = 4 if warp % 8 == 0 else 1
    core = 2 if warp % 2 == 0 else 1
    return (warp // (x * core), x, core, weft // zlo, zlo)


def solution(mesh):
    fine = Mesh(mesh.devices.reshape(factors(mesh)), WARP + WEFT)
    field = P(None, None, WARP, WEFT)
    placed = (field, field, P(None, WARP, WEFT), P(None, WARP, WEFT), P(WARP, WEFT), P(), P(), P())
    return jax.shard_map(
        shards,
        mesh=fine,
        in_specs=placed,
        out_specs=(field, field, P(), P(), P()),
        check_vma=False,
    )
```

profile of v0, /device:TPU:1, one launch (start us, length us, event | category | flops | bytes accessed | tf_op | source)
XLA Modules:
  0.0 107.5 jit_solution(13071863045263034831)
XLA Ops:
  0.6 1.6 %pack_tile.1 = (f32[8,24,128]{2,1,0:T(8,128)}, f32[24,128]{1,0:T(8,128)}, f32[24,128]{1,0:T(8,128)}, f32[1,24,128]{2,1,0:T(8,128)}) custom-call(f32[1,8,8,128]{3,2,1,0:T(8,128)} %state_hbm.1, f32[1,8,8,128]{3,2,1,0:T(8,128)} %adjoint_hbm.1, f32[2,8,128]{2,1,0:T(8,128)} %stiff_hbm.1, s32[1,8,128]{2,1,0:T(8,128)} %pinned_hbm.1, s32[8,128]{1,0:T(8,128)} %weave_hbm.1, ...), custom_call_target="tpu_custom_call" | custom-call | tf_op jit(solution)/shard_map/pack_tile/pallas_call | solution.py:519
  2.2 4.4 %collective-permute-start = (f32[24,128]{1,0:T(8,128)}, f32[24,128]{1,0:T(8,128)S(1)}, u32[]{:S(2)}, u32[]{:S(2)}) collective-permute-start(f32[24,128]{1,0:T(8,128)} %get-tuple-element.16), channel_id=1, source_target_pairs={{0,1},{1,2},{2,3},{3,4},{4,5},{5,6},{6,7},{7,8},{8,9},{9,10},{10,1... | collective-permute-start | bytes 36872 | tf_op jit(solution)/shard_map/ppermute | solution.py:536
  6.6 1.3 %collective-permute-start.1 = (f32[24,128]{1,0:T(8,128)}, f32[24,128]{1,0:T(8,128)S(1)}, u32[]{:S(2)}, u32[]{:S(2)}) collective-permute-start(f32[24,128]{1,0:T(8,128)} %get-tuple-element.17), channel_id=1, source_target_pairs={{1,0},{2,1},{3,2},{4,3},{5,4},{6,5},{7,6},{8,7},{9,8},{10,9},{11,1... | collective-permute-start | bytes 36872 | tf_op jit(solution)/shard_map/ppermute | solution.py:536
  7.9 0.0 collective-permute-done
  7.9 3.5 %collective-permute-done.1 = f32[24,128]{1,0:T(8,128)S(1)} collective-permute-done((f32[24,128]{1,0:T(8,128)}, f32[24,128]{1,0:T(8,128)S(1)}, u32[]{:S(2)}, u32[]{:S(2)}) %collective-permute-start.1) | collective-permute-done | bytes 12320 | tf_op jit(solution)/shard_map/ppermute | solution.py:536
  11.4 0.9 pad_maximum_fusion.1.own_ref
  12.3 0.0 copy-start.2
  12.4 6.8 %collective-permute-start.2 = (f32[11,24,128]{2,1,0:T(8,128)S(1)}, f32[11,24,128]{2,1,0:T(8,128)S(1)}, u32[]{:S(2)}, u32[]{:S(2)}) collective-permute-start(f32[11,24,128]{2,1,0:T(8,128)S(1)} %pad_maximum_fusion.1.own_ref), channel_id=1, source_target_pairs={{0,16},{16,0},{32,48},{48,32},{64,80},{80,64},{96,112},{112,96},{1... | collective-permute-start | bytes 405512 | tf_op jit(solution)/shard_map/ppermute | solution.py:570
  19.2 0.1 pad.8.clone
  19.3 0.9 collective-permute-done.2.partner_ref
  20.1 0.1 maximum_maximum_fusion
  20.2 0.0 copy-done.2
  20.2 0.0 copy-start
  20.2 2.1 %collective-permute-start.3 = (f32[12,24,128]{2,1,0:T(8,128)S(1)}, f32[12,24,128]{2,1,0:T(8,128)S(1)}, u32[]{:S(2)}, u32[]{:S(2)}) collective-permute-start(f32[12,24,128]{2,1,0:T(8,128)S(1)} %pad_maximum_fusion), channel_id=1, source_target_pairs={{16,32},{32,16},{48,64},{64,48},{80,96},{96,80},{112,128},{128,112... | collective-permute-start | bytes 442376 | tf_op jit(solution)/shard_map/ppermute | solution.py:575
  22.3 4.5 %collective-permute-done.3.cross_ref = f32[12,24,128]{2,1,0:T(8,128)S(1)} collective-permute-done((f32[12,24,128]{2,1,0:T(8,128)S(1)}, f32[12,24,128]{2,1,0:T(8,128)S(1)}, u32[]{:S(2)}, u32[]{:S(2)}) %collective-permute-start.3) | collective-permute-done | bytes 147488 | tf_op jit(solution)/shard_map/ppermute | solution.py:575
  26.8 0.0 copy-start.1
  26.8 1.9 %collective-permute-start.4 = (f32[4,8,128]{2,1,0:T(8,128)S(1)}, f32[4,8,128]{2,1,0:T(8,128)S(1)}, u32[]{:S(2)}, u32[]{:S(2)}) collective-permute-start(f32[4,8,128]{2,1,0:T(8,128)S(1)} %pad_maximum_fusion.2), channel_id=1, source_target_pairs={{0,16},{16,0},{32,48},{48,32},{64,80},{80,64},{96,112},{112,96},{1... | collective-permute-start | bytes 49160 | tf_op jit(solution)/shard_map/ppermute | solution.py:577
  28.8 1.1 %collective-permute-done.4.far_ref = f32[4,8,128]{2,1,0:T(8,128)S(1)} collective-permute-done((f32[4,8,128]{2,1,0:T(8,128)S(1)}, f32[4,8,128]{2,1,0:T(8,128)S(1)}, u32[]{:S(2)}, u32[]{:S(2)}) %collective-permute-start.4) | collective-permute-done | bytes 16416 | tf_op jit(solution)/shard_map/ppermute | solution.py:577
  29.9 0.0 copy-done
  29.9 0.0 copy-done.1
  29.9 10.7 %substeps.1 = (f32[1,8,8,128]{3,2,1,0:T(8,128)}, f32[1,8,8,128]{3,2,1,0:T(8,128)}, f32[32,9,2,128]{3,2,1,0:T(2,128)S(1)}) custom-call(f32[11,24,128]{2,1,0:T(8,128)S(1)} %pad_maximum_fusion.1.own_ref, s32[1]{0:T(128)} %bitcast.3.core_ref, f32[11,24,128]{2,1,0:T(8,128)S(1)} %collective-permute-done.2.partner_ref, ...), custom_call_target="tpu_custom_call" | custom-call | tf_op jit(solution)/shard_map/substeps/pallas_call | solution.py:503
  40.7 24.3 %all_to_all.15 = f32[32,9,2,128]{3,2,1,0:T(2,128)S(1)} all-to-all(f32[32,9,2,128]{3,2,1,0:T(2,128)S(1)} %get-tuple-element.21), channel_id=1, replica_groups=mesh['zhi'=4,'x'=4,'core'=2,'y'=4,'zlo'=4] {'x','core','y'}, dimensions={0} | all-to-all | bytes 589824 | tf_op jit(solution)/shard_map/all_to_all | solution.py:541
  65.0 0.1 reduce_sum.18
  65.1 25.3 %all_to_all.16 = f32[16,9,2,128]{3,2,1,0:T(2,128)S(1)} all-to-all(f32[16,9,2,128]{3,2,1,0:T(2,128)S(1)} %broadcast_in_dim.18), channel_id=1, replica_groups=mesh['zhi'=4,'x'=4,'core'=2,'y'=4,'zlo'=4] {'zhi','zlo'}, dimensions={0} | all-to-all | bytes 294912 | tf_op jit(solution)/shard_map/all_to_all | solution.py:543
  90.5 0.1 reduce_sum.19
  90.5 0.1 broadcast_in_dim.19
  90.6 16.0 %all_to_all.17.flat_ref = f32[32,9,2,128]{3,2,1,0:T(2,128)S(1)} all-to-all(f32[32,9,2,128]{3,2,1,0:T(2,128)S(1)} %broadcast_in_dim.19), channel_id=1, replica_groups=mesh['zhi'=4,'x'=4,'core'=2,'y'=4,'zlo'=4] {'x','core','y'}, dimensions={0} | all-to-all | bytes 589824 | tf_op jit(solution)/shard_map/all_to_all | solution.py:545
  106.6 0.9 unpack_grads.1
  (6 shorter events, 0.1 us)
Async XLA Ops:
  2.2 5.7 %collective-permute-start = (f32[24,128]{1,0:T(8,128)}, f32[24,128]{1,0:T(8,128)S(1)}, u32[]{:S(2)}, u32[]{:S(2)}) collective-permute-start(f32[24,128]{1,0:T(8,128)} %get-tuple-element.16), channel_id=1, source_target_pairs={{0,1},{1,2},{2,3},{3,4},{4,5},{5,6},{6,7},{7,8},{8,9},{9,10},{10,1... | collective-permute-start | bytes 36872 | tf_op jit(solution)/shard_map/ppermute | solution.py:536
  6.6 4.8 %collective-permute-start.1 = (f32[24,128]{1,0:T(8,128)}, f32[24,128]{1,0:T(8,128)S(1)}, u32[]{:S(2)}, u32[]{:S(2)}) collective-permute-start(f32[24,128]{1,0:T(8,128)} %get-tuple-element.17), channel_id=1, source_target_pairs={{1,0},{2,1},{3,2},{4,3},{5,4},{6,5},{7,6},{8,7},{9,8},{10,9},{11,1... | collective-permute-start | bytes 36872 | tf_op jit(solution)/shard_map/ppermute | solution.py:536
  12.3 7.9 %copy-start.2 = (f32[8,24,128]{2,1,0:T(8,128)S(1)}, f32[8,24,128]{2,1,0:T(8,128)}, u32[]{:S(2)}) copy-start(f32[8,24,128]{2,1,0:T(8,128)} %get-tuple-element.15) | copy-start | bytes 294916
  12.4 7.8 %collective-permute-start.2 = (f32[11,24,128]{2,1,0:T(8,128)S(1)}, f32[11,24,128]{2,1,0:T(8,128)S(1)}, u32[]{:S(2)}, u32[]{:S(2)}) collective-permute-start(f32[11,24,128]{2,1,0:T(8,128)S(1)} %pad_maximum_fusion.1.own_ref), channel_id=1, source_target_pairs={{0,16},{16,0},{32,48},{48,32},{64,80},{80,64},{96,112},{112,96},{1... | collective-permute-start | bytes 405512 | tf_op jit(solution)/shard_map/ppermute | solution.py:570
  20.2 9.7 %copy-start = (bf16[256,256]{1,0:T(8,128)(2,1)S(1)}, bf16[256,256]{1,0:T(8,128)(2,1)}, u32[]{:S(2)}) copy-start(bf16[256,256]{1,0:T(8,128)(2,1)} %second_weight_ref.1) | copy-start | bytes 393220
  20.2 6.6 %collective-permute-start.3 = (f32[12,24,128]{2,1,0:T(8,128)S(1)}, f32[12,24,128]{2,1,0:T(8,128)S(1)}, u32[]{:S(2)}, u32[]{:S(2)}) collective-permute-start(f32[12,24,128]{2,1,0:T(8,128)S(1)} %pad_maximum_fusion), channel_id=1, source_target_pairs={{16,32},{32,16},{48,64},{64,48},{80,96},{96,80},{112,128},{128,112... | collective-permute-start | bytes 442376 | tf_op jit(solution)/shard_map/ppermute | solution.py:575
  26.8 3.1 %copy-start.1 = (bf16[12,256]{1,0:T(8,128)(2,1)S(1)}, bf16[12,256]{1,0:T(8,128)(2,1)}, u32[]{:S(2)}) copy-start(bf16[12,256]{1,0:T(8,128)(2,1)} %first_weight_ref.1) | copy-start | bytes 18436
  26.8 3.1 %collective-permute-start.4 = (f32[4,8,128]{2,1,0:T(8,128)S(1)}, f32[4,8,128]{2,1,0:T(8,128)S(1)}, u32[]{:S(2)}, u32[]{:S(2)}) collective-permute-start(f32[4,8,128]{2,1,0:T(8,128)S(1)} %pad_maximum_fusion.2), channel_id=1, source_target_pairs={{0,16},{16,0},{32,48},{48,32},{64,80},{80,64},{96,112},{112,96},{1... | collective-permute-start | bytes 49160 | tf_op jit(solution)/shard_map/ppermute | solution.py:577
where the time goes:
time: 108 us
  blocking collectives  65.7 us (61%)
  starting transfers between devices  16.4 us (15%)
  Pallas kernels  13.2 us (12%)
  waiting for transfers between devices  10.1 us (9%)
  other arithmetic  1.18 us (1%)
    all_to_all x1, blocking collectives, sum_everywhere(): part = jnp.sum(lax.all_to_all(part, COLUMN, 0, 0, tiled=True), axis=0)  25.3 us
    all_to_all x1, blocking collectives, sum_everywhere(): part = jnp.sum(lax.all_to_all(part, PLANE, 0, 0, tiled=True), axis=0)  24.3 us
    all_to_all x1, blocking collectives, sum_everywhere(): return lax.all_to_all(part, PLANE, 0, 0, tiled=True)  16 us
    pallas_call x1, Pallas kernels, run_main(): pl.pallas_call(main_kernel, out_shape=(jax.ShapeDtypeStruct((1, 8, TILE_R...  10.7 us
    ppermute x1, starting transfers between devices, shards(): partner = lax.ppermute(own, WARP, mates)  6.8 us
    ppermute x2, starting transfers between devices, shift(): lax.ppermute(value, axis, [(i, i + step) for i in range(count) if 0 <= i...  5.66 us
    ppermute x1, waiting for transfers between devices, shards(): cross = lax.ppermute(wide, WARP, pairs)  4.52 us
    ppermute x2, waiting for transfers between devices, shift(): lax.ppermute(value, axis, [(i, i + step) for i in range(count) if 0 <= i...  3.53 us
  transfers between devices with their start and end apart: 5, of which 4 were waited for; matrix products, arithmetic and copies ran while one was open for 0% of the time, Pallas kernels for 0%

commit v1 on v0

--- a/solution.py
+++ b/solution.py
@@ -527,8 +527,9 @@
         in_specs=[pl.BlockSpec(memory_space=pltpu.HBM)] * 6,
         scratch_shapes=[pltpu.VMEM(value.shape, value.dtype) for value in operands]
         + [pltpu.SemaphoreType.DMA((6,))],
+        compiler_params=pltpu.CompilerParams(vmem_limit_bytes=4 << 20),
         name="pack_tile",
-    )(*operands)
+    )(*[pltpu.with_memory_space_constraint(value, pltpu.HBM) for value in operands])
 
 
 def shift(value, axis, step):

time: 108 us -> 106 us (0.981)
  no operation moved by 1% of the time
where the time goes in v1:
time: 106 us
  blocking collectives  65.7 us (62%)
  starting transfers between devices  16.3 us (15%)
  Pallas kernels  12.6 us (12%)
  waiting for transfers between devices  9.85 us (9%)
    all_to_all x1, blocking collectives, sum_everywhere(): part = jnp.sum(lax.all_to_all(part, COLUMN, 0, 0, tiled=True), axis=0)  25.3 us
    all_to_all x1, blocking collectives, sum_everywhere(): part = jnp.sum(lax.all_to_all(part, PLANE, 0, 0, tiled=True), axis=0)  24.3 us
    all_to_all x1, blocking collectives, sum_everywhere(): return lax.all_to_all(part, PLANE, 0, 0, tiled=True)  16 us
    pallas_call x1, Pallas kernels, run_main(): pl.pallas_call(main_kernel, out_shape=(jax.ShapeDtypeStruct((1, 8, TILE_R...  10.7 us
    ppermute x1, starting transfers between devices, shards(): partner = lax.ppermute(own, WARP, mates)  6.67 us
    ppermute x2, starting transfers between devices, shift(): lax.ppermute(value, axis, [(i, i + step) for i in range(count) if 0 <= i...  5.66 us
    ppermute x1, waiting for transfers between devices, shards(): cross = lax.ppermute(wide, WARP, pairs)  4.52 us
    ppermute x2, waiting for transfers between devices, shift(): lax.ppermute(value, axis, [(i, i + step) for i in range(count) if 0 <= i...  3.32 us
  transfers between devices with their start and end apart: 5, of which 4 were waited for; matrix products, arithmetic and copies ran while one was open for 0% of the time, Pallas kernels for 0%

profile of v1, /device:TPU:1, one launch (start us, length us, event | category | flops | bytes accessed | tf_op | source)
XLA Modules:
  0.0 105.6 jit_solution(17346052508884494348)
XLA Ops:
  0.6 1.0 pack_tile.1
  1.6 4.4 %collective-permute-start = (f32[24,128]{1,0:T(8,128)S(1)}, f32[24,128]{1,0:T(8,128)S(1)}, u32[]{:S(2)}, u32[]{:S(2)}) collective-permute-start(f32[24,128]{1,0:T(8,128)S(1)} %get-tuple-element.16), channel_id=1, source_target_pairs={{0,1},{1,2},{2,3},{3,4},{4,5},{5,6},{6,7},{7,8},{8,9},{9,10},{10,1... | collective-permute-start | bytes 36872 | tf_op jit(solution)/shard_map/ppermute | solution.py:537
  6.0 1.3 %collective-permute-start.1 = (f32[24,128]{1,0:T(8,128)S(1)}, f32[24,128]{1,0:T(8,128)S(1)}, u32[]{:S(2)}, u32[]{:S(2)}) collective-permute-start(f32[24,128]{1,0:T(8,128)S(1)} %get-tuple-element.17), channel_id=1, source_target_pairs={{1,0},{2,1},{3,2},{4,3},{5,4},{6,5},{7,6},{8,7},{9,8},{10,9},{11,1... | collective-permute-start | bytes 36872 | tf_op jit(solution)/shard_map/ppermute | solution.py:537
  7.3 0.0 collective-permute-done
  7.3 3.3 %collective-permute-done.1 = f32[24,128]{1,0:T(8,128)S(1)} collective-permute-done((f32[24,128]{1,0:T(8,128)S(1)}, f32[24,128]{1,0:T(8,128)S(1)}, u32[]{:S(2)}, u32[]{:S(2)}) %collective-permute-start.1) | collective-permute-done | bytes 12320 | tf_op jit(solution)/shard_map/ppermute | solution.py:537
  10.6 6.7 %collective-permute-start.2 = (f32[11,24,128]{2,1,0:T(8,128)S(1)}, f32[11,24,128]{2,1,0:T(8,128)S(1)}, u32[]{:S(2)}, u32[]{:S(2)}) collective-permute-start(f32[11,24,128]{2,1,0:T(8,128)S(1)} %pad_maximum_fusion.1.own_ref), channel_id=1, source_target_pairs={{0,16},{16,0},{32,48},{48,32},{64,80},{80,64},{96,112},{112,96},{1... | collective-permute-start | bytes 405512 | tf_op jit(solution)/shard_map/ppermute | solution.py:571
  17.3 0.1 pad.8.clone
  17.4 0.9 collective-permute-done.2.partner_ref
  18.3 0.1 maximum_maximum_fusion
  18.3 0.0 copy-start
  18.4 2.1 %collective-permute-start.3 = (f32[12,24,128]{2,1,0:T(8,128)S(1)}, f32[12,24,128]{2,1,0:T(8,128)S(1)}, u32[]{:S(2)}, u32[]{:S(2)}) collective-permute-start(f32[12,24,128]{2,1,0:T(8,128)S(1)} %pad_maximum_fusion), channel_id=1, source_target_pairs={{16,32},{32,16},{48,64},{64,48},{80,96},{96,80},{112,128},{128,112... | collective-permute-start | bytes 442376 | tf_op jit(solution)/shard_map/ppermute | solution.py:576
  20.4 4.5 %collective-permute-done.3.cross_ref = f32[12,24,128]{2,1,0:T(8,128)S(1)} collective-permute-done((f32[12,24,128]{2,1,0:T(8,128)S(1)}, f32[12,24,128]{2,1,0:T(8,128)S(1)}, u32[]{:S(2)}, u32[]{:S(2)}) %collective-permute-start.3) | collective-permute-done | bytes 147488 | tf_op jit(solution)/shard_map/ppermute | solution.py:576
  25.0 0.0 copy-start.1
  25.0 1.9 %collective-permute-start.4 = (f32[4,8,128]{2,1,0:T(8,128)S(1)}, f32[4,8,128]{2,1,0:T(8,128)S(1)}, u32[]{:S(2)}, u32[]{:S(2)}) collective-permute-start(f32[4,8,128]{2,1,0:T(8,128)S(1)} %pad_maximum_fusion.2), channel_id=1, source_target_pairs={{0,16},{16,0},{32,48},{48,32},{64,80},{80,64},{96,112},{112,96},{1... | collective-permute-start | bytes 49160 | tf_op jit(solution)/shard_map/ppermute | solution.py:578
  26.9 1.1 %collective-permute-done.4.far_ref = f32[4,8,128]{2,1,0:T(8,128)S(1)} collective-permute-done((f32[4,8,128]{2,1,0:T(8,128)S(1)}, f32[4,8,128]{2,1,0:T(8,128)S(1)}, u32[]{:S(2)}, u32[]{:S(2)}) %collective-permute-start.4) | collective-permute-done | bytes 16416 | tf_op jit(solution)/shard_map/ppermute | solution.py:578
  28.1 0.0 copy-done
  28.1 0.0 copy-done.1
  28.1 10.7 %substeps.1 = (f32[1,8,8,128]{3,2,1,0:T(8,128)}, f32[1,8,8,128]{3,2,1,0:T(8,128)}, f32[32,9,2,128]{3,2,1,0:T(2,128)S(1)}) custom-call(f32[11,24,128]{2,1,0:T(8,128)S(1)} %pad_maximum_fusion.1.own_ref, s32[1]{0:T(128)} %bitcast.3.core_ref, f32[11,24,128]{2,1,0:T(8,128)S(1)} %collective-permute-done.2.partner_ref, ...), custom_call_target="tpu_custom_call" | custom-call | tf_op jit(solution)/shard_map/substeps/pallas_call | solution.py:503
  38.8 24.3 %all_to_all.15 = f32[32,9,2,128]{3,2,1,0:T(2,128)S(1)} all-to-all(f32[32,9,2,128]{3,2,1,0:T(2,128)S(1)} %get-tuple-element.21), channel_id=1, replica_groups=mesh['zhi'=4,'x'=4,'core'=2,'y'=4,'zlo'=4] {'x','core','y'}, dimensions={0} | all-to-all | bytes 589824 | tf_op jit(solution)/shard_map/all_to_all | solution.py:542
  63.1 0.1 reduce_sum.18
  63.3 25.3 %all_to_all.16 = f32[16,9,2,128]{3,2,1,0:T(2,128)S(1)} all-to-all(f32[16,9,2,128]{3,2,1,0:T(2,128)S(1)} %broadcast_in_dim.18), channel_id=1, replica_groups=mesh['zhi'=4,'x'=4,'core'=2,'y'=4,'zlo'=4] {'zhi','zlo'}, dimensions={0} | all-to-all | bytes 294912 | tf_op jit(solution)/shard_map/all_to_all | solution.py:544
  88.6 0.1 reduce_sum.19
  88.7 0.1 broadcast_in_dim.19
  88.7 16.0 %all_to_all.17.flat_ref = f32[32,9,2,128]{3,2,1,0:T(2,128)S(1)} all-to-all(f32[32,9,2,128]{3,2,1,0:T(2,128)S(1)} %broadcast_in_dim.19), channel_id=1, replica_groups=mesh['zhi'=4,'x'=4,'core'=2,'y'=4,'zlo'=4] {'x','core','y'}, dimensions={0} | all-to-all | bytes 589824 | tf_op jit(solution)/shard_map/all_to_all | solution.py:546
  104.8 0.9 unpack_grads.1
  (7 shorter events, 0.1 us)
Async XLA Ops:
  1.6 5.7 %collective-permute-start = (f32[24,128]{1,0:T(8,128)S(1)}, f32[24,128]{1,0:T(8,128)S(1)}, u32[]{:S(2)}, u32[]{:S(2)}) collective-permute-start(f32[24,128]{1,0:T(8,128)S(1)} %get-tuple-element.16), channel_id=1, source_target_pairs={{0,1},{1,2},{2,3},{3,4},{4,5},{5,6},{6,7},{7,8},{8,9},{9,10},{10,1... | collective-permute-start | bytes 36872 | tf_op jit(solution)/shard_map/ppermute | solution.py:537
  6.0 4.6 %collective-permute-start.1 = (f32[24,128]{1,0:T(8,128)S(1)}, f32[24,128]{1,0:T(8,128)S(1)}, u32[]{:S(2)}, u32[]{:S(2)}) collective-permute-start(f32[24,128]{1,0:T(8,128)S(1)} %get-tuple-element.17), channel_id=1, source_target_pairs={{1,0},{2,1},{3,2},{4,3},{5,4},{6,5},{7,6},{8,7},{9,8},{10,9},{11,1... | collective-permute-start | bytes 36872 | tf_op jit(solution)/shard_map/ppermute | solution.py:537
  10.6 7.6 %collective-permute-start.2 = (f32[11,24,128]{2,1,0:T(8,128)S(1)}, f32[11,24,128]{2,1,0:T(8,128)S(1)}, u32[]{:S(2)}, u32[]{:S(2)}) collective-permute-start(f32[11,24,128]{2,1,0:T(8,128)S(1)} %pad_maximum_fusion.1.own_ref), channel_id=1, source_target_pairs={{0,16},{16,0},{32,48},{48,32},{64,80},{80,64},{96,112},{112,96},{1... | collective-permute-start | bytes 405512 | tf_op jit(solution)/shard_map/ppermute | solution.py:571
  18.3 9.7 %copy-start = (bf16[256,256]{1,0:T(8,128)(2,1)S(1)}, bf16[256,256]{1,0:T(8,128)(2,1)}, u32[]{:S(2)}) copy-start(bf16[256,256]{1,0:T(8,128)(2,1)} %second_weight_ref.1) | copy-start | bytes 393220
  18.4 6.6 %collective-permute-start.3 = (f32[12,24,128]{2,1,0:T(8,128)S(1)}, f32[12,24,128]{2,1,0:T(8,128)S(1)}, u32[]{:S(2)}, u32[]{:S(2)}) collective-permute-start(f32[12,24,128]{2,1,0:T(8,128)S(1)} %pad_maximum_fusion), channel_id=1, source_target_pairs={{16,32},{32,16},{48,64},{64,48},{80,96},{96,80},{112,128},{128,112... | collective-permute-start | bytes 442376 | tf_op jit(solution)/shard_map/ppermute | solution.py:576
  25.0 3.1 %copy-start.1 = (bf16[12,256]{1,0:T(8,128)(2,1)S(1)}, bf16[12,256]{1,0:T(8,128)(2,1)}, u32[]{:S(2)}) copy-start(bf16[12,256]{1,0:T(8,128)(2,1)} %first_weight_ref.1) | copy-start | bytes 18436
  25.0 3.1 %collective-permute-start.4 = (f32[4,8,128]{2,1,0:T(8,128)S(1)}, f32[4,8,128]{2,1,0:T(8,128)S(1)}, u32[]{:S(2)}, u32[]{:S(2)}) collective-permute-start(f32[4,8,128]{2,1,0:T(8,128)S(1)} %pad_maximum_fusion.2), channel_id=1, source_target_pairs={{0,16},{16,0},{32,48},{48,32},{64,80},{80,64},{96,112},{112,96},{1... | collective-permute-start | bytes 49160 | tf_op jit(solution)/shard_map/ppermute | solution.py:578

commit v2 on v1

--- a/solution.py
+++ b/solution.py
@@ -229,33 +229,28 @@
 
     first_core = core_ref[0] == 0
 
-    def pick(lower, upper, at):
-        return jnp.where(first_core, lower[at], upper[at])
+    def cross_at(i, part, skip):
+        if i >= TILE_ROWS:
+            return cross_ref[22 + 3 * (i - TILE_ROWS) + part]
+        if part == 1:
+            return cross_ref[16 + min(max(i - skip, 0), 5)]
+        return cross_ref[i + 4 * part]
 
     def received(e, part):
         at = slice(8 * part, 8 * part + 8)
         if e < -TILE_ROWS:
             i = e + TILE_ROWS + 2
-            return [
-                jnp.where(first_core, cross_ref[n, p, :], far_ref[m])
-                for (n, p), m in zip(extra(i), (i, 2, 3))
-            ]
+            return [jnp.where(first_core, cross_ref[28 + m], far_ref[m]) for m in (i, 2, 3)]
         if e < 0:
-            return [pick(cross_ref, partner_ref, (i, at)) for i in (e + TILE_ROWS, TILE_ROWS, TILE_ROWS + 1)]
+            places = (e + TILE_ROWS, TILE_ROWS, TILE_ROWS + 1)
+            return [jnp.where(first_core, cross_at(i, part, 2), partner_ref[i, at]) for i in places]
         if e < TILE_ROWS:
             return [own_ref[i, at, :] for i in (e, TILE_ROWS, TILE_ROWS + 1)]
         if e < 2 * TILE_ROWS:
-            return [pick(partner_ref, cross_ref, (i, at)) for i in (e - TILE_ROWS, TILE_ROWS, TILE_ROWS + 1)]
+            places = (e - TILE_ROWS, TILE_ROWS, TILE_ROWS + 1)
+            return [jnp.where(first_core, partner_ref[i, at], cross_at(i, part, 0)) for i in places]
         i = e - 2 * TILE_ROWS
-        return [
-            jnp.where(first_core, far_ref[m], cross_ref[n, p, :])
-            for (n, p), m in zip(extra(i), (i, 2, 3))
-        ]
-
-    def extra(i):
-        n = TILE_ROWS + 2
-        row = (n, slice(8 * i, 8 * i + 8))
-        return row, (n, slice(16, 24)), (n + 1, slice(0, 8))
+        return [jnp.where(first_core, far_ref[m], cross_ref[28 + m]) for m in (i, 2, 3)]
 
     for row in range(ALL_ROWS):
         e = row - FIRST
@@ -570,12 +565,16 @@
     mates = [(i, i ^ 1) for i in range(count)]
     partner = lax.ppermute(own, WARP, mates)
     outward = lax.dynamic_slice_in_dim(partner, core * (TILE_ROWS - 2), 2, axis=0)[:, 0:8]
-    tail = jnp.concatenate([outward, partner[TILE_ROWS : TILE_ROWS + 2, 0:8], jnp.zeros((2, 8, LANES), F32)], axis=0)
-    wide = jnp.concatenate([own[: TILE_ROWS + 2], tail.reshape(2, 24, LANES)], axis=0)
+    parts = own[:TILE_ROWS].reshape(TILE_ROWS, 3, 8, LANES)
+    near = lax.dynamic_slice_in_dim(parts[:, 1], core * 2, 6, axis=0)
+    sides = [left.reshape(3, 8, LANES), right.reshape(3, 8, LANES)]
+    wide = jnp.concatenate(
+        [parts[:, 0], parts[:, 2], near, *sides, outward, partner[TILE_ROWS : TILE_ROWS + 2, 0:8]], axis=0
+    )
     pairs = [(i, j) for i in range(count) for j in [((i + 1) ^ 1) - 1] if 0 <= j < count]
     cross = lax.ppermute(wide, WARP, pairs)
-    inward = lax.dynamic_slice_in_dim(cross, (1 - core) * (TILE_ROWS - 2), 2, axis=0)[:, 0:8]
-    far = lax.ppermute(jnp.concatenate([inward, cross[TILE_ROWS : TILE_ROWS + 2, 0:8]], axis=0), WARP, mates)
+    inward = lax.dynamic_slice_in_dim(cross, (1 - core) * (TILE_ROWS - 2), 2, axis=0)
+    far = lax.ppermute(jnp.concatenate([inward, cross[22:23], cross[25:26]], axis=0), WARP, mates)
 
     final_state, state_adjoint, grads = run_main(
         own, core.reshape(1), partner, cross, far, first_weight, second_weight

time: 106 us -> 105 us (level)
  no operation moved by 1% of the time
where the time goes in v2:
time: 105 us
  blocking collectives  65.2 us (62%)
  starting transfers between devices  16.3 us (16%)
  Pallas kernels  12.6 us (12%)
  waiting for transfers between devices  9.67 us (9%)
    all_to_all x1, blocking collectives, sum_everywhere(): part = jnp.sum(lax.all_to_all(part, COLUMN, 0, 0, tiled=True), axis=0)  25.4 us
    all_to_all x1, blocking collectives, sum_everywhere(): part = jnp.sum(lax.all_to_all(part, PLANE, 0, 0, tiled=True), axis=0)  23.7 us
    all_to_all x1, blocking collectives, sum_everywhere(): return lax.all_to_all(part, PLANE, 0, 0, tiled=True)  16 us
    pallas_call x1, Pallas kernels, run_main(): pl.pallas_call(main_kernel, out_shape=(jax.ShapeDtypeStruct((1, 8, TILE_R...  10.7 us
    ppermute x1, starting transfers between devices, shards(): partner = lax.ppermute(own, WARP, mates)  6.8 us
    ppermute x2, starting transfers between devices, shift(): lax.ppermute(value, axis, [(i, i + step) for i in range(count) if 0 <= i...  5.66 us
    ppermute x1, waiting for transfers between devices, shards(): cross = lax.ppermute(wide, WARP, pairs)  4.35 us
    ppermute x2, waiting for transfers between devices, shift(): lax.ppermute(value, axis, [(i, i + step) for i in range(count) if 0 <= i...  3.23 us
  transfers between devices with their start and end apart: 5, of which 4 were waited for; matrix products, arithmetic and copies ran while one was open for 0% of the time, Pallas kernels for 0%

profile of v2, /device:TPU:1, one launch (start us, length us, event | category | flops | bytes accessed | tf_op | source)
XLA Modules:
  0.0 104.9 jit_solution(7588167479054193901)
XLA Ops:
  0.6 1.0 pack_tile.1
  1.6 4.4 %collective-permute-start = (f32[24,128]{1,0:T(8,128)S(1)}, f32[24,128]{1,0:T(8,128)S(1)}, u32[]{:S(2)}, u32[]{:S(2)}) collective-permute-start(f32[24,128]{1,0:T(8,128)S(1)} %get-tuple-element.16), channel_id=1, source_target_pairs={{0,1},{1,2},{2,3},{3,4},{4,5},{5,6},{6,7},{7,8},{8,9},{9,10},{10,1... | collective-permute-start | bytes 36872 | tf_op jit(solution)/shard_map/ppermute | solution.py:532
  6.0 1.3 %collective-permute-start.1 = (f32[24,128]{1,0:T(8,128)S(1)}, f32[24,128]{1,0:T(8,128)S(1)}, u32[]{:S(2)}, u32[]{:S(2)}) collective-permute-start(f32[24,128]{1,0:T(8,128)S(1)} %get-tuple-element.17), channel_id=1, source_target_pairs={{1,0},{2,1},{3,2},{4,3},{5,4},{6,5},{7,6},{8,7},{9,8},{10,9},{11,1... | collective-permute-start | bytes 36872 | tf_op jit(solution)/shard_map/ppermute | solution.py:532
  7.4 0.0 collective-permute-done
  7.4 3.2 %collective-permute-done.1 = f32[24,128]{1,0:T(8,128)S(1)} collective-permute-done((f32[24,128]{1,0:T(8,128)S(1)}, f32[24,128]{1,0:T(8,128)S(1)}, u32[]{:S(2)}, u32[]{:S(2)}) %collective-permute-start.1) | collective-permute-done | bytes 12320 | tf_op jit(solution)/shard_map/ppermute | solution.py:532
  10.6 0.0 copy-start
  10.6 6.8 %collective-permute-start.2 = (f32[11,24,128]{2,1,0:T(8,128)S(1)}, f32[11,24,128]{2,1,0:T(8,128)S(1)}, u32[]{:S(2)}, u32[]{:S(2)}) collective-permute-start(f32[11,24,128]{2,1,0:T(8,128)S(1)} %pad_maximum_fusion.own_ref), channel_id=1, source_target_pairs={{0,16},{16,0},{32,48},{48,32},{64,80},{80,64},{96,112},{112,96},{1... | collective-permute-start | bytes 405512 | tf_op jit(solution)/shard_map/ppermute | solution.py:566
  17.5 0.9 collective-permute-done.2.partner_ref
  18.4 1.9 %collective-permute-start.3 = (f32[32,8,128]{2,1,0:T(8,128)S(1)}, f32[32,8,128]{2,1,0:T(8,128)S(1)}, u32[]{:S(2)}, u32[]{:S(2)}) collective-permute-start(f32[32,8,128]{2,1,0:T(8,128)S(1)} %constant_dynamic-update-slice_fusion), channel_id=1, source_target_pairs={{16,32},{32,16},{48,64},{64,48},{80,96},{96,80},{112,128},{128,112... | collective-permute-start | bytes 393224 | tf_op jit(solution)/shard_map/ppermute | solution.py:575
  20.3 4.3 %collective-permute-done.3.cross_ref = f32[32,8,128]{2,1,0:T(8,128)S(1)} collective-permute-done((f32[32,8,128]{2,1,0:T(8,128)S(1)}, f32[32,8,128]{2,1,0:T(8,128)S(1)}, u32[]{:S(2)}, u32[]{:S(2)}) %collective-permute-start.3) | collective-permute-done | bytes 131104 | tf_op jit(solution)/shard_map/ppermute | solution.py:575
  24.7 0.0 copy-start.1
  24.7 1.9 %collective-permute-start.4 = (f32[4,8,128]{2,1,0:T(8,128)S(1)}, f32[4,8,128]{2,1,0:T(8,128)S(1)}, u32[]{:S(2)}, u32[]{:S(2)}) collective-permute-start(f32[4,8,128]{2,1,0:T(8,128)S(1)} %pad_maximum_fusion.1), channel_id=1, source_target_pairs={{0,16},{16,0},{32,48},{48,32},{64,80},{80,64},{96,112},{112,96},{1... | collective-permute-start | bytes 49160 | tf_op jit(solution)/shard_map/ppermute | solution.py:577
  26.6 1.1 %collective-permute-done.4.far_ref = f32[4,8,128]{2,1,0:T(8,128)S(1)} collective-permute-done((f32[4,8,128]{2,1,0:T(8,128)S(1)}, f32[4,8,128]{2,1,0:T(8,128)S(1)}, u32[]{:S(2)}, u32[]{:S(2)}) %collective-permute-start.4) | collective-permute-done | bytes 16416 | tf_op jit(solution)/shard_map/ppermute | solution.py:577
  27.8 0.0 copy-done
  27.8 0.0 copy-done.1
  27.8 10.7 %substeps.1 = (f32[1,8,8,128]{3,2,1,0:T(8,128)}, f32[1,8,8,128]{3,2,1,0:T(8,128)}, f32[32,9,2,128]{3,2,1,0:T(2,128)S(1)}) custom-call(f32[11,24,128]{2,1,0:T(8,128)S(1)} %pad_maximum_fusion.own_ref, s32[1]{0:T(128)} %bitcast.3.core_ref, f32[11,24,128]{2,1,0:T(8,128)S(1)} %collective-permute-done.2.partner_ref, ...), custom_call_target="tpu_custom_call" | custom-call | tf_op jit(solution)/shard_map/substeps/pallas_call | solution.py:498
  38.5 23.7 %all_to_all.15 = f32[32,9,2,128]{3,2,1,0:T(2,128)S(1)} all-to-all(f32[32,9,2,128]{3,2,1,0:T(2,128)S(1)} %get-tuple-element.21), channel_id=1, replica_groups=mesh['zhi'=4,'x'=4,'core'=2,'y'=4,'zlo'=4] {'x','core','y'}, dimensions={0} | all-to-all | bytes 589824 | tf_op jit(solution)/shard_map/all_to_all | solution.py:537
  62.2 0.1 reduce_sum.18
  62.4 25.4 %all_to_all.16 = f32[16,9,2,128]{3,2,1,0:T(2,128)S(1)} all-to-all(f32[16,9,2,128]{3,2,1,0:T(2,128)S(1)} %broadcast_in_dim.14), channel_id=1, replica_groups=mesh['zhi'=4,'x'=4,'core'=2,'y'=4,'zlo'=4] {'zhi','zlo'}, dimensions={0} | all-to-all | bytes 294912 | tf_op jit(solution)/shard_map/all_to_all | solution.py:539
  87.8 0.1 reduce_sum.19
  87.9 0.1 broadcast_in_dim.15
  87.9 16.0 %all_to_all.17.flat_ref = f32[32,9,2,128]{3,2,1,0:T(2,128)S(1)} all-to-all(f32[32,9,2,128]{3,2,1,0:T(2,128)S(1)} %broadcast_in_dim.15), channel_id=1, replica_groups=mesh['zhi'=4,'x'=4,'core'=2,'y'=4,'zlo'=4] {'x','core','y'}, dimensions={0} | all-to-all | bytes 589824 | tf_op jit(solution)/shard_map/all_to_all | solution.py:541
  104.0 0.9 unpack_grads.1
  (13 shorter events, 0.1 us)
Async XLA Ops:
  1.6 5.8 %collective-permute-start = (f32[24,128]{1,0:T(8,128)S(1)}, f32[24,128]{1,0:T(8,128)S(1)}, u32[]{:S(2)}, u32[]{:S(2)}) collective-permute-start(f32[24,128]{1,0:T(8,128)S(1)} %get-tuple-element.16), channel_id=1, source_target_pairs={{0,1},{1,2},{2,3},{3,4},{4,5},{5,6},{6,7},{7,8},{8,9},{9,10},{10,1... | collective-permute-start | bytes 36872 | tf_op jit(solution)/shard_map/ppermute | solution.py:532
  6.0 4.6 %collective-permute-start.1 = (f32[24,128]{1,0:T(8,128)S(1)}, f32[24,128]{1,0:T(8,128)S(1)}, u32[]{:S(2)}, u32[]{:S(2)}) collective-permute-start(f32[24,128]{1,0:T(8,128)S(1)} %get-tuple-element.17), channel_id=1, source_target_pairs={{1,0},{2,1},{3,2},{4,3},{5,4},{6,5},{7,6},{8,7},{9,8},{10,9},{11,1... | collective-permute-start | bytes 36872 | tf_op jit(solution)/shard_map/ppermute | solution.py:532
  10.6 17.2 %copy-start = (bf16[256,256]{1,0:T(8,128)(2,1)S(1)}, bf16[256,256]{1,0:T(8,128)(2,1)}, u32[]{:S(2)}) copy-start(bf16[256,256]{1,0:T(8,128)(2,1)} %second_weight_ref.1) | copy-start | bytes 393220
  10.6 7.8 %collective-permute-start.2 = (f32[11,24,128]{2,1,0:T(8,128)S(1)}, f32[11,24,128]{2,1,0:T(8,128)S(1)}, u32[]{:S(2)}, u32[]{:S(2)}) collective-permute-start(f32[11,24,128]{2,1,0:T(8,128)S(1)} %pad_maximum_fusion.own_ref), channel_id=1, source_target_pairs={{0,16},{16,0},{32,48},{48,32},{64,80},{80,64},{96,112},{112,96},{1... | collective-permute-start | bytes 405512 | tf_op jit(solution)/shard_map/ppermute | solution.py:566
  18.4 6.3 %collective-permute-start.3 = (f32[32,8,128]{2,1,0:T(8,128)S(1)}, f32[32,8,128]{2,1,0:T(8,128)S(1)}, u32[]{:S(2)}, u32[]{:S(2)}) collective-permute-start(f32[32,8,128]{2,1,0:T(8,128)S(1)} %constant_dynamic-update-slice_fusion), channel_id=1, source_target_pairs={{16,32},{32,16},{48,64},{64,48},{80,96},{96,80},{112,128},{128,112... | collective-permute-start | bytes 393224 | tf_op jit(solution)/shard_map/ppermute | solution.py:575
  24.7 3.1 %copy-start.1 = (bf16[12,256]{1,0:T(8,128)(2,1)S(1)}, bf16[12,256]{1,0:T(8,128)(2,1)}, u32[]{:S(2)}) copy-start(bf16[12,256]{1,0:T(8,128)(2,1)} %first_weight_ref.1) | copy-start | bytes 18436
  24.7 3.1 %collective-permute-start.4 = (f32[4,8,128]{2,1,0:T(8,128)S(1)}, f32[4,8,128]{2,1,0:T(8,128)S(1)}, u32[]{:S(2)}, u32[]{:S(2)}) collective-permute-start(f32[4,8,128]{2,1,0:T(8,128)S(1)} %pad_maximum_fusion.1), channel_id=1, source_target_pairs={{0,16},{16,0},{32,48},{48,32},{64,80},{80,64},{96,112},{112,96},{1... | collective-permute-start | bytes 49160 | tf_op jit(solution)/shard_map/ppermute | solution.py:577
